TPU v7x, 512 devices: a whole 4x4x16 slice. The times are simulated.
512 devices in a mesh: clip: 64 (over z, y_lo, core), disc: 8 (over y_hi, x).
Axes of the slice: x: 4, y: 4 (y_hi: 2, y_lo: 2; y = y_hi * 2 + y_lo), z: 16, core: 2. Of those that a mesh axis runs over, the one named last changes fastest.
Arguments:
- waveform: bfloat16 [64, 2, 32768], P('clip', None, 'disc'), may hold values from -3 to 3
- window_length: int32 [8], P('disc'), may hold values from 256 to 1024
- first_weight: bfloat16 [8, 1024, 512], P('disc'), may hold values from -0.1875 to 0.1875
- first_bias: float32 [8, 512], P('disc'), may hold values from -2 to 2
- head_weight: bfloat16 [8, 512], P('disc'), may hold values from -0.25 to 0.25
Outputs:
- waveform_grad: float32 [64, 2, 32768], P('clip', None, 'disc')
- first_grad: float32 [8, 1024, 512], P('disc', 'clip')
- head_grad: float32 [8, 512, 2], P('disc', 'clip')
Inputs may be any that keep to these rules, and one draw needn't show every extreme that they name: `window_length`: each branch's window length in samples, centred in a frame of 1024.
All inputs are finite; a program needn't handle non-finite values.
Results may differ from a plain program's by a relative error of at most 0.04.
Values may be sent and summed in bfloat16 or wider, within the bound.
A program may use at most 64 MiB of HBM per device.

v0:
```python
import math

import jax
import jax.numpy as jnp
from jax import lax
from jax.sharding import PartitionSpec as P

GEN_WEIGHT = 10.0
LEAK = 0.2


def make_table(length, frame):
    positions = jnp.arange(frame, dtype=jnp.int32)
    shifted = positions - (frame - length) // 2
    inside = (shifted >= 0) & (shifted < length)
    phases = 2.0 * jnp.pi * shifted.astype(jnp.float32) / length.astype(jnp.float32)
    window = jnp.where(inside, 0.5 - 0.5 * jnp.cos(phases), 0.0)
    column = jnp.arange(frame // 2, dtype=jnp.int32)
    angles = (
        2.0 * jnp.pi * (positions[:, None] * column[None, :] % frame).astype(jnp.float32) / frame
    )
    factor = window[:, None] / math.sqrt(frame)
    return jnp.concatenate([jnp.cos(angles) * factor, -jnp.sin(angles) * factor], axis=1).astype(
        jnp.bfloat16
    )


def make_frames(signal, hop_size):
    length = signal.shape[-1]
    frame_count = length // hop_size
    leading = signal.shape[:-1]
    padded = jnp.pad(signal, [(0, 0)] * len(leading) + [(2 * hop_size, hop_size)])
    blocks = padded.reshape(leading + (frame_count + 3, hop_size))
    return jnp.concatenate(
        [blocks[..., offset : offset + frame_count, :] for offset in range(4)], axis=-1
    )


def intersection_add(frame_delta, hop_size):
    frame_count = frame_delta.shape[-2]
    leading = frame_delta.shape[:-2]
    pieces = frame_delta.reshape(leading + (frame_count, 4, hop_size))
    summed = jnp.zeros(leading + (frame_count + 3, hop_size), jnp.float32)
    for offset in range(4):
        padding = [(0, 0)] * len(leading) + [(offset, 3 - offset), (0, 0)]
        summed = summed + jnp.pad(pieces[..., offset, :], padding)
    return summed[..., 2 : frame_count + 2, :].reshape(leading + (frame_count * hop_size,))


def forward_part(rows, table, weight, bias, head):
    spectrum = jnp.dot(rows, table, preferred_element_type=jnp.float32).astype(jnp.bfloat16)
    preact = jnp.dot(spectrum, weight, preferred_element_type=jnp.float32) + bias[None, :]
    slopes = jnp.where(preact > 0, 1.0, LEAK)
    hidden = (preact * slopes).astype(jnp.bfloat16)
    logits = jnp.dot(hidden, head, preferred_element_type=jnp.float32)
    head_wide = head.astype(jnp.float32)[None, :]
    disc_delta = (logits[:, None] * head_wide * slopes).astype(jnp.bfloat16)
    gen_delta = (GEN_WEIGHT * (logits - 1.0)[:, None] * head_wide * slopes).astype(jnp.bfloat16)
    head_terms = jnp.stack(
        [
            jnp.sum(logits[:, None] * hidden.astype(jnp.float32), axis=0),
            jnp.sum(disc_delta.astype(jnp.float32), axis=0),
        ],
        axis=1,
    )
    return (spectrum, disc_delta, gen_delta, head_terms)


def weight_product(spectrum, disc_delta):
    return lax.dot_general(
        spectrum, disc_delta, (((0,), (0,)), ((), ())), preferred_element_type=jnp.float32
    )


def generator_back(gen_delta, weight, table):
    spec_delta = jnp.dot(gen_delta, weight.T, preferred_element_type=jnp.float32).astype(
        jnp.bfloat16
    )
    return jnp.dot(spec_delta, table.T, preferred_element_type=jnp.float32)


def body(waveform, window_length, first_weight, first_bias, head_weight):
    whole = lax.all_gather(waveform, "disc", axis=2, tiled=True)
    frame = first_weight.shape[1]
    hop_size = frame // 4
    rows = make_frames(whole, hop_size).reshape(-1, frame)
    branch = 0
    table = make_table(window_length[branch], frame)
    spectrum, disc_delta, gen_delta, head_terms = forward_part(
        rows, table, first_weight[branch], first_bias[branch], head_weight[branch]
    )
    tables = [table]
    gen_deltas = [gen_delta]
    head_list = [head_terms]
    heads = jnp.stack(head_list)
    branch = 0
    frame_delta = generator_back(gen_deltas[branch], first_weight[branch], tables[branch])
    frame_delta = frame_delta.reshape(whole.shape[:2] + (-1, frame))
    summed = intersection_add(frame_delta, hop_size)
    waveform_grad = lax.psum_scatter(
        summed.astype(jnp.bfloat16), "disc", scatter_dimension=2, tiled=True
    ).astype(jnp.float32)
    full_grad = jnp.stack([weight_product(spectrum, disc_delta)])
    first_grad, head_grad = (
        lax.psum_scatter(full_grad, "clip", scatter_dimension=1, tiled=True),
        lax.psum_scatter(heads, "clip", scatter_dimension=1, tiled=True),
    )
    return (waveform_grad, first_grad, head_grad)


def solution(mesh):
    placed = (
        P("clip", None, "disc"),
        P("disc"),
        P("disc", None, None),
        P("disc", None),
        P("disc", None),
    )
    return jax.shard_map(
        body,
        mesh=mesh,
        in_specs=placed,
        out_specs=(P("clip", None, "disc"), P("disc", "clip", None), P("disc", "clip", None)),
        check_vma=False,
    )
```

profile of v0, /device:TPU:2, one launch (start us, length us, event | category | flops | bytes accessed | tf_op | source)
XLA Modules:
  0.0 472.7 jit_solution(17468436289232926810)
XLA Ops:
  7.2 0.0 copy-start
  7.2 0.0 reduce-scatter.8.cloned.1.call-start
  8.0 0.7 reduce
  8.7 34.7 %all_gather.3 = bf16[1,2,32768]{2,1,0:T(2,128)(2,1)S(1)} all-gather(bf16[1,2,4096]{2,1,0:T(2,128)(2,1)} %param.5), channel_id=1, replica_groups=mesh['clip'=64,'disc'=8] {'disc'}, dimensions={2}, use_global_device_ids=true | all-gather | bytes 147456 | tf_op jit(solution)/shard_map/all_gather | solution.py:83
  43.4 0.1 pad.20
  43.5 0.2 reshape.45
  43.7 0.1 fusion.44
  43.8 0.1 select_multiply_fusion.3
  43.9 8.8 %multiply_convert_fusion.1 = (bf16[1024,512]{1,0:T(8,128)(2,1)S(1)}, bf16[1024,512]{1,0:T(8,128)(2,1)S(1)}) fusion(f32[1024]{0:T(1024)S(1)} %select_multiply_fusion.3), kind=kLoop, calls=%fused_computation.10 | loop fusion | flops 9961472 | bytes 2101248 | tf_op jit(solution)/shard_map/convert.2
  52.7 0.0 copy-start.1
  52.7 0.1 pad_maximum_fusion.5
  52.8 0.0 copy-start.3
  52.8 0.7 fusion.8
  53.5 0.2 copy-done.1
  53.7 0.0 copy-start.2
  53.7 0.0 copy-done
  53.7 0.0 copy-done.3
  53.7 0.5 broadcast_compare_fusion
  54.2 0.2 copy-done.2
  54.4 0.2 fusion.31
  54.6 3.3 fusion.6
  57.9 1.7 reshape_reshape.3
  59.6 0.8 slice_bitcast_fusion.3
  60.4 1.1 fusion.26
  61.5 25.4 %copy.17 = bf16[1,2,32768]{1,0,2:T(2,128)(2,1)} copy(bf16[1,2,32768]{2,1,0:T(2,128)(2,1)S(1)} %convert_element_type.71) | data formatting | bytes 262144
  86.9 10.6 %copy.26 = bf16[32768,1,2]{2,0,1:T(8,128)(2,1)} copy(bf16[32768,1,2]{2,1,0:T(2,128)(2,1)} %bitcast.52) | data formatting | bytes 262144
  97.5 0.0 reduce-scatter.8.cloned.1.call-update
  97.5 0.0 reduce-scatter.6.cloned.1.call-start
  97.5 1.9 convolution_bitcast_fusion
  99.4 0.0 reduce-scatter.6.cloned.1.call-update
  99.5 1.3 dynamic-slice
  101.4 0.2 multiply_reduce_fusion
  101.6 111.7 %all-reduce.5 = f32[1,512,2]{1,2,0:T(2,128)S(1)} all-reduce(f32[1,512,2]{1,2,0:T(2,128)S(1)} %maximum_bitcast_fusion), channel_id=4, replica_groups=mesh['clip'=64,'disc'=8] {'clip'}, use_global_device_ids=true, to_apply=%region_4.5.clone | all-reduce | flops 1024 | bytes 8192
  213.3 0.6 constant_dynamic-slice_fusion
  213.9 17.5 %reduce-scatter.8.cloned.1.call-done = bf16[4096,2]{1,0:T(8,128)(2,1)} async-done(((bf16[32768,2]{1,0:T(8,128)(2,1)}), bf16[4096,2]{1,0:T(8,128)(2,1)}) %reduce-scatter.8.cloned.1.call-update) | async-done | bytes 16400
  231.4 2.8 reshape_bitcast_fusion
  234.2 2.0 copy.18
  236.1 0.6 convert_element_type.72
  236.8 229.1 %reduce-scatter.6.cloned.1.call-done = f32[1,16,512]{2,1,0:T(8,128)} async-done(((f32[1,1024,512]{2,1,0:T(8,128)}), f32[1,16,512]{2,1,0:T(8,128)}) %reduce-scatter.6.cloned.1.call-update) | async-done | bytes 32784 | tf_op jit(solution)/shard_map/reduce_scatter | solution.py:105
  (4 shorter events, 0.1 us)
Async XLA Ops:
  7.2 46.6 %copy-start = (bf16[1,1024,512]{2,1,0:T(8,128)(2,1)S(1)}, bf16[1,1024,512]{2,1,0:T(8,128)(2,1)}, u32[]{:S(2)}) copy-start(bf16[1,1024,512]{2,1,0:T(8,128)(2,1)} %param.7) | copy-start | bytes 3145732
  7.2 224.2 %reduce-scatter.8.cloned.1.call-start = ((), (), s32[]{:S(2)}) async-start(), calls=%async_computation.3 | async-start | bytes 9437184
  52.7 1.0 copy-start.1
  52.8 0.9 copy-start.3
  53.7 0.7 copy-start.2
  97.5 368.4 %reduce-scatter.6.cloned.1.call-start = ((), (), s32[]{:S(2)}) async-start(), calls=%async_computation.2 | async-start | bytes 2129920 | tf_op jit(solution)/shard_map/reduce_scatter | solution.py:105
Sparse Core Ops, SparseCore 0:
  97.6 133.7 reduce-scatter.7
  234.7 231.1 reduce-scatter.5
where the time goes:
time: 473 us
  waiting for transfers between devices  247 us (52%)
  blocking collectives  146 us (31%)
  local copies, waits for them, and re-layouts  46 us (10%)
  between operations  15.6 us (3%)
  other arithmetic  11.5 us (2%)
  matrix products  6.53 us (1%)
    reduce_scatter x1, waiting for transfers between devices, body(): lax.psum_scatter(full_grad, 'clip', scatter_dimension=1, tiled=True)  229 us
    unnamed x1, blocking collectives  112 us
    unnamed x14, local copies, waits for them, and re-layouts  43.1 us
    all_gather x1, blocking collectives, body(): whole = lax.all_gather(waveform, 'disc', axis=2, tiled=True)  34.7 us
    unnamed x3, waiting for transfers between devices  17.5 us
  transfers between devices with their start and end apart: 2, of which 2 were waited for; matrix products, arithmetic and copies ran while one was open for 2% of the time, Pallas kernels for 0%

commit v1 on v0

v1 whole, which is shorter than its diff:
```python
import math

import jax
import jax.numpy as jnp
import numpy as np
from jax import lax
from jax.experimental import pallas as pl
from jax.experimental.pallas import tpu as pltpu
from jax.sharding import PartitionSpec as P

GEN_WEIGHT = 10.0
LEAK = 0.2
MESH = pl.DeviceIdType.MESH
GROUP = 16
X_SIZE = 4
Z_SIZE = 16
F32 = jnp.float32
BF16 = jnp.bfloat16


def twiddles(frame):
    column = np.arange(frame // 2)
    coarse = (np.arange(0, frame, GROUP)[:, None] * column[None, :]) % frame
    fine = (np.arange(GROUP)[:, None] * column[None, :]) % frame
    angle = 2.0 * np.pi / frame
    coarse = np.concatenate([np.cos(coarse * angle), np.sin(coarse * angle)], axis=0)
    fine = np.concatenate([np.cos(fine * angle), np.sin(fine * angle)], axis=0)
    return coarse[:, None, :].astype(np.float32), fine.astype(np.float32)


def remote(src, dst, send_sem, recv_sem, device):
    return pltpu.make_async_remote_copy(
        src_ref=src,
        dst_ref=dst,
        send_sem=send_sem,
        recv_sem=recv_sem,
        device_id=device,
        device_id_type=MESH,
    )


def kernel(
    wave,
    length_ref,
    coarse_hbm,
    fine_hbm,
    weight_hbm,
    bias,
    head,
    out_wave,
    out_first,
    out_head,
    gathered,
    coarse,
    fine,
    weight,
    table,
    padded,
    rows,
    spectrum,
    preact,
    disc_delta,
    gen_delta,
    spec_delta,
    grad,
    grad_low,
    core_in,
    kept,
    pair_out,
    pair_in,
    z_out,
    z_in,
    heads,
    heads_mid,
    heads_all,
    core_heads,
    pair_heads,
    zh_out,
    zh_in,
    wave_sum,
    wave_low,
    x_in,
    y_out,
    y_in,
    local_sem,
    gather_send,
    gather_recv,
    core_send,
    core_recv,
    pair_send,
    pair_recv,
    z_send,
    z_recv,
    zh_send,
    zh_recv,
    wave_send,
    wave_recv,
):
    clip = lax.axis_index("clip")
    disc = lax.axis_index("disc")
    core = lax.rem(clip, 2)
    y_lo = lax.rem(clip // 2, 2)
    z = clip // 4
    inner = lax.rem(clip, 4)
    x = lax.rem(disc, X_SIZE)
    y_hi = disc // X_SIZE
    frame, hidden_size = weight.shape
    half = frame // 2
    hop = frame // 4
    frames = padded.shape[1] - 16
    shard = wave.shape[1]
    lanes = 128
    steps = Z_SIZE // 2

    core_peer = {"clip": clip + 1 - 2 * core}
    pair_peer = {"clip": clip + 2 - 4 * y_lo}
    z_up = {"clip": lax.rem(z + 1, Z_SIZE) * 4 + inner}
    z_down = {"clip": lax.rem(z + Z_SIZE - 1, Z_SIZE) * 4 + inner}
    other = lax.rem(disc + X_SIZE, 2 * X_SIZE)
    y_peer = {"disc": other}
    x_at = [lax.rem(x + k, X_SIZE) for k in range(X_SIZE)]
    x_peer = [{"disc": y_hi * X_SIZE + at} for at in x_at]

    coarse_copy = pltpu.make_async_copy(coarse_hbm, coarse, local_sem.at[0])
    fine_copy = pltpu.make_async_copy(fine_hbm, fine, local_sem.at[1])
    weight_copy = pltpu.make_async_copy(weight_hbm, weight, local_sem.at[2])
    barrier = pltpu.get_barrier_semaphore()
    peers = [y_peer, x_peer[2], x_peer[1], x_peer[3], z_up, z_down, pair_peer, core_peer]
    for peer in peers:
        pl.semaphore_signal(barrier, inc=1, device_id=peer, device_id_type=MESH)
    coarse_copy.start()
    fine_copy.start()
    weight_copy.start()
    gathered[disc] = wave[...]
    padded[:, 0:8, :] = jnp.zeros((2, 8, hop), F32)
    padded[:, frames + 8 : frames + 16, :] = jnp.zeros((2, 8, hop), F32)
    pl.semaphore_wait(barrier, len(peers))

    def gather_copy(slot, src, at, peer):
        return remote(src, gathered.at[at], gather_send.at[slot], gather_recv.at[slot], peer)

    to_y = gather_copy(0, wave, disc, y_peer)
    to_x = [gather_copy(k, wave, disc, x_peer[k]) for k in (2, 1, 3)]
    for copy in [to_y] + to_x:
        copy.start()

    coarse_copy.wait()
    fine_copy.wait()
    length = length_ref[0]
    start = lax.shift_right_arithmetic(frame - length, 1)
    length_float = length.astype(F32)
    groups = frame // GROUP

    def table_rows(g):
        row = pl.multiple_of(g * GROUP, GROUP)
        position = lax.broadcasted_iota(jnp.int32, (GROUP, lanes), 0) + (row - start)
        inside = (position >= 0) & (position < length)
        phase = 2.0 * jnp.pi * position.astype(F32) / length_float
        window = jnp.where(inside, 0.5 - 0.5 * jnp.cos(phase), 0.0)
        factor = window * (1.0 / math.sqrt(frame))
        for q in range(half // lanes):
            at = slice(q * lanes, (q + 1) * lanes)
            cos_a = coarse[g, :, at]
            sin_a = coarse[groups + g, :, at]
            cos_b = fine[0:GROUP, at]
            sin_b = fine[GROUP : 2 * GROUP, at]
            real = (cos_a * cos_b - sin_a * sin_b) * factor
            imag = -(sin_a * cos_b + cos_a * sin_b) * factor
            table[pl.ds(row, GROUP), at] = real.astype(BF16)
            table[pl.ds(row, GROUP), half + q * lanes : half + (q + 1) * lanes] = imag.astype(BF16)

    pl.loop(0, groups // 2)(table_rows)
    to_y.wait_recv()
    forward = [gather_copy(3 + k, gathered.at[other], other, x_peer[k]) for k in (2, 1, 3)]
    for copy in forward:
        copy.start()
    pl.loop(groups // 2, groups)(table_rows)
    for copy in to_x + forward:
        copy.wait_recv()

    for j in range(2 * X_SIZE):
        for ch in range(2):
            padded[ch, 8 + shard * j : 8 + shard * (j + 1), :] = gathered[j, ch].astype(F32)
    for piece in range(4):
        for ch in range(2):
            rows[ch * frames : (ch + 1) * frames, piece * hop : (piece + 1) * hop] = padded[
                ch, 6 + piece : 6 + piece + frames, :
            ].astype(BF16)
    for n in range(4):
        at = slice(n * hop, (n + 1) * hop)
        spectrum[:, at] = jnp.dot(rows[...], table[:, at], preferred_element_type=F32).astype(BF16)
    weight_copy.wait()
    preact[...] = jnp.dot(spectrum[...], weight[...], preferred_element_type=F32)
    head_wide = head[...].astype(F32)
    step = 32

    def delta_rows(i, sums):
        at = pl.ds(pl.multiple_of(i * step, step), step)
        pre = preact[at, :] + bias[...]
        slopes = jnp.where(pre > 0, 1.0, LEAK)
        hidden = (pre * slopes).astype(BF16).astype(F32)
        logits = jnp.sum(hidden * head_wide, axis=1, keepdims=True)
        disc_low = (logits * head_wide * slopes).astype(BF16)
        disc_delta[at, :] = disc_low
        gen_delta[at, :] = (GEN_WEIGHT * (logits - 1.0) * head_wide * slopes).astype(BF16)
        return (
            sums[0] + jnp.sum(logits * hidden, axis=0, keepdims=True),
            sums[1] + jnp.sum(disc_low.astype(F32), axis=0, keepdims=True),
        )

    zero = jnp.zeros((1, hidden_size), F32)
    sums = lax.fori_loop(0, 2 * frames // step, delta_rows, (zero, zero))
    for r in range(hidden_size // lanes):
        for t in range(2):
            heads[r, t : t + 1, :] = sums[t][:, r * lanes : (r + 1) * lanes]

    for n in range(4):
        at = slice(n * hop, (n + 1) * hop)
        part = lax.dot_general(
            spectrum[:, at], disc_delta[...], (((0,), (0,)), ((), ())), preferred_element_type=F32
        ).reshape(Z_SIZE // 4, 2, 2, GROUP, hidden_size)
        grad[n * 4 : (n + 1) * 4] = part
        grad_low[n * 4 : (n + 1) * 4] = part.astype(BF16)

    def target(i):
        s = i // 2
        return lax.rem(z + Z_SIZE // 2 + s + lax.rem(i, 2) * (Z_SIZE - 1 - 2 * s), Z_SIZE)

    def core_copy(i):
        return remote(
            grad_low.at[target(i), :, 1 - core],
            core_in.at[i],
            core_send.at[i],
            core_recv.at[i],
            core_peer,
        )

    def pair_copy(i):
        return remote(pair_out.at[i], pair_in.at[i], pair_send.at[i], pair_recv.at[i], pair_peer)

    core_heads_copy = remote(
        heads, core_heads, core_send.at[Z_SIZE], core_recv.at[Z_SIZE], core_peer
    )
    pair_heads_copy = remote(
        heads_mid, pair_heads, pair_send.at[Z_SIZE], pair_recv.at[Z_SIZE], pair_peer
    )
    core_heads_copy.start()
    pl.loop(0, Z_SIZE)(lambda i: core_copy(i).start())

    spec_delta[...] = lax.dot_general(
        gen_delta[...], weight[...], (((1,), (1,)), ((), ())), preferred_element_type=F32
    ).astype(BF16)
    for piece in (2, 0, 1, 3):
        back = lax.dot_general(
            spec_delta[...],
            table[piece * hop : (piece + 1) * hop, :],
            (((1,), (1,)), ((), ())),
            preferred_element_type=F32,
        ).reshape(2, frames, hop)
        at = slice(6 + piece, 6 + piece + frames)
        if piece == 2:
            wave_sum[:, at, :] = back
        else:
            wave_sum[:, at, :] = wave_sum[:, at, :] + back

    core_heads_copy.wait_recv()
    heads_mid[...] = heads[...] + core_heads[...]
    pair_heads_copy.start()

    @pl.loop(0, Z_SIZE)
    def _(i):
        core_copy(i).wait_recv()
        at = target(i)
        pair_out[i] = (grad[at, 1 - y_lo, core] + core_in[i, 1 - y_lo].astype(F32)).astype(BF16)
        pair_copy(i).start()
        kept[i] = grad[at, y_lo, core] + core_in[i, y_lo].astype(F32)

    for j in range(2 * X_SIZE):
        for ch in range(2):
            wave_low[j // X_SIZE, j % X_SIZE, ch] = wave_sum[
                ch, 8 + shard * j : 8 + shard * (j + 1), :
            ].astype(BF16)

    def x_copy(k):
        return remote(
            wave_low.at[:, x_at[k]],
            x_in.at[k - 1],
            wave_send.at[k - 1],
            wave_recv.at[k - 1],
            x_peer[k],
        )

    y_copy = remote(y_out, y_in, wave_send.at[3], wave_recv.at[3], y_peer)
    for k in (2, 1, 3):
        x_copy(k).start()

    pair_heads_copy.wait_recv()
    heads_all[...] = heads_mid[...] + pair_heads[...]

    def z_copy(i, peer):
        return remote(z_out.at[i], z_in.at[i], z_send.at[i], z_recv.at[i], peer)

    def zh_copy(i, peer):
        return remote(zh_out.at[i], zh_in.at[i], zh_send.at[i], zh_recv.at[i], peer)

    for s in range(steps):
        for up, peer in ((0, z_down), (1, z_up)):
            i = 2 * s + up
            pair_copy(i).wait_recv()
            total = kept[i] + pair_in[i].astype(F32)
            total_heads = heads_all[target(i) // 4]
            if s > 0:
                z_copy(i - 2, peer).wait_recv()
                zh_copy(i - 2, peer).wait_recv()
                total = total + z_in[i - 2].astype(F32)
                total_heads = total_heads + zh_in[i - 2]
            if i == Z_SIZE - 1:
                last, last_heads = total, total_heads
            else:
                z_out[i] = total.astype(BF16)
                z_copy(i, peer).start()
                zh_out[i] = total_heads
                zh_copy(i, peer).start()
        if s == 1:
            for k in (2, 1, 3):
                x_copy(k).wait_recv()

            def x_sum(at):
                total = wave_low[at, x].astype(F32)
                for k in range(3):
                    total = total + x_in[k, at].astype(F32)
                return total

            y_out[...] = x_sum(1 - y_hi).astype(BF16)
            y_copy.start()
            out_wave[...] = x_sum(y_hi)
        if s == 4:
            y_copy.wait_recv()
            out_wave[...] = out_wave[...] + y_in[...].astype(F32)

    i = Z_SIZE - 2
    z_copy(i, z_down).wait_recv()
    zh_copy(i, z_down).wait_recv()
    out_first[...] = last + z_in[i].astype(F32)
    width = 2 * hidden_size // (4 * Z_SIZE * 2)
    shift = lax.rem(lanes - width * lax.rem(clip, lanes // width), lanes)
    total_heads = last_heads + zh_in[i]
    out_head[...] = pltpu.roll(jnp.concatenate([total_heads] * 4, axis=0), shift, axis=1)

    for copy in [to_y] + to_x + forward:
        copy.wait_send()
    core_heads_copy.wait_send()
    pair_heads_copy.wait_send()

    @pl.loop(0, Z_SIZE)
    def _(i):
        core_copy(i).wait_send()
        pair_copy(i).wait_send()

    for i in range(Z_SIZE - 1):
        z_copy(i, z_up).wait_send()
        zh_copy(i, z_up).wait_send()
    for k in (2, 1, 3):
        x_copy(k).wait_send()
    y_copy.wait_send()


def body(waveform, window_length, first_weight, first_bias, head_weight):
    frame, hidden_size = first_weight.shape[1:]
    hop = frame // 4
    shard = waveform.shape[2] // hop
    frames = shard * 2 * X_SIZE
    count = 2 * frames
    block = (GROUP, hidden_size)
    vmem = pl.BlockSpec(memory_space=pltpu.VMEM)
    any_space = pl.BlockSpec(memory_space=pl.ANY)
    coarse, fine = [jnp.asarray(part) for part in twiddles(frame)]
    out_wave, out_first, out_head = pl.pallas_call(
        kernel,
        out_shape=(
            jax.ShapeDtypeStruct((2, shard, hop), F32),
            jax.ShapeDtypeStruct(block, F32),
            jax.ShapeDtypeStruct((8, 128), F32),
        ),
        in_specs=[
            vmem,
            pl.BlockSpec(memory_space=pltpu.SMEM),
            any_space,
            any_space,
            any_space,
            vmem,
            vmem,
        ],
        out_specs=(vmem, vmem, vmem),
        scratch_shapes=[
            pltpu.VMEM((2 * X_SIZE, 2, shard, hop), BF16),
            pltpu.VMEM(coarse.shape, F32),
            pltpu.VMEM(fine.shape, F32),
            pltpu.VMEM((frame, hidden_size), BF16),
            pltpu.VMEM((frame, frame), BF16),
            pltpu.VMEM((2, frames + 16, hop), F32),
            pltpu.VMEM((count, frame), BF16),
            pltpu.VMEM((count, frame), BF16),
            pltpu.VMEM((count, hidden_size), F32),
            pltpu.VMEM((count, hidden_size), BF16),
            pltpu.VMEM((count, hidden_size), BF16),
            pltpu.VMEM((count, frame), BF16),
            pltpu.VMEM((Z_SIZE, 2, 2) + block, F32),
            pltpu.VMEM((Z_SIZE, 2, 2) + block, BF16),
            pltpu.VMEM((Z_SIZE, 2) + block, BF16),
            pltpu.VMEM((Z_SIZE,) + block, F32),
            pltpu.VMEM((Z_SIZE,) + block, BF16),
            pltpu.VMEM((Z_SIZE,) + block, BF16),
            pltpu.VMEM((Z_SIZE,) + block, BF16),
            pltpu.VMEM((Z_SIZE,) + block, BF16),
            pltpu.VMEM((hidden_size // 128, 2, 128), F32),
            pltpu.VMEM((hidden_size // 128, 2, 128), F32),
            pltpu.VMEM((hidden_size // 128, 2, 128), F32),
            pltpu.VMEM((hidden_size // 128, 2, 128), F32),
            pltpu.VMEM((hidden_size // 128, 2, 128), F32),
            pltpu.VMEM((Z_SIZE, 2, 128), F32),
            pltpu.VMEM((Z_SIZE, 2, 128), F32),
            pltpu.VMEM((2, frames + 16, hop), F32),
            pltpu.VMEM((2, X_SIZE, 2, shard, hop), BF16),
            pltpu.VMEM((3, 2, 2, shard, hop), BF16),
            pltpu.VMEM((2, shard, hop), BF16),
            pltpu.VMEM((2, shard, hop), BF16),
            pltpu.SemaphoreType.DMA((3,)),
            pltpu.SemaphoreType.DMA((7,)),
            pltpu.SemaphoreType.DMA((7,)),
            pltpu.SemaphoreType.DMA((Z_SIZE + 1,)),
            pltpu.SemaphoreType.DMA((Z_SIZE + 1,)),
            pltpu.SemaphoreType.DMA((Z_SIZE + 1,)),
            pltpu.SemaphoreType.DMA((Z_SIZE + 1,)),
            pltpu.SemaphoreType.DMA((Z_SIZE,)),
            pltpu.SemaphoreType.DMA((Z_SIZE,)),
            pltpu.SemaphoreType.DMA((Z_SIZE,)),
            pltpu.SemaphoreType.DMA((Z_SIZE,)),
            pltpu.SemaphoreType.DMA((4,)),
            pltpu.SemaphoreType.DMA((4,)),
        ],
        compiler_params=pltpu.CompilerParams(
            collective_id=0, has_side_effects=True, vmem_limit_bytes=48 * 1024 * 1024
        ),
    )(
        waveform.reshape(2, shard, hop),
        window_length,
        coarse,
        fine,
        first_weight[0],
        first_bias,
        head_weight,
    )
    width = 8
    return (
        out_wave.reshape(1, 2, shard * hop),
        out_first[None],
        out_head[:2, :width].T[None],
    )


def solution(mesh):
    placed = (
        P("clip", None, "disc"),
        P("disc"),
        P("disc", None, None),
        P("disc", None),
        P("disc", None),
    )
    return jax.shard_map(
        body,
        mesh=mesh,
        in_specs=placed,
        out_specs=(P("clip", None, "disc"), P("disc", "clip", None), P("disc", "clip", None)),
        check_vma=False,
    )
```

time: 473 us -> 58.9 us (0.12)
  the two profiles are of different devices: /device:TPU:2 before, /device:TPU:16 now
where the time goes in v1:
time: 58.9 us; the launch traced here: 58.6 us
  Pallas kernels  51.7 us (88%)
  local copies, waits for them, and re-layouts  5.57 us (9%)
  between operations  1.31 us (2%)
    pallas_call x1, Pallas kernels, body(): pl.pallas_call(kernel, out_shape=(jax.ShapeDtypeStruct((2, shard, hop), F...  51.7 us
    unnamed x12, local copies, waits for them, and re-layouts  4.37 us

profile of v1, /device:TPU:16, one launch (start us, length us, event | category | flops | bytes accessed | tf_op | source)
XLA Modules:
  0.0 58.6 jit_solution(963659829309718575)
XLA Ops:
  1.3 0.0 copy-start.3
  1.3 0.0 copy-start.4
  1.3 0.7 %copy.12 = bf16[1,2,16,256]{3,2,1,0:T(8,128)(2,1)S(1)} copy(bf16[1,2,16,256]{3,1,2,0:T(2,128)(2,1)} %bitcast.14) | data formatting | bytes 32768
  2.0 0.0 copy-done.3
  2.0 0.0 copy-done.4
  2.0 0.0 copy-start
  2.0 1.2 %copy-done = bf16[1,1024,512]{2,1,0:T(8,128)(2,1)S(1)} copy-done((bf16[1,1024,512]{2,1,0:T(8,128)(2,1)S(1)}, bf16[1,1024,512]{2,1,0:T(8,128)(2,1)}, u32[]{:S(2)}) %copy-start) | copy-done | bytes 1048600
  3.3 0.0 copy-start.1
  3.3 0.9 %copy-done.1 = f32[128,1,512]{2,1,0:T(1,128)S(1)} copy-done((f32[128,1,512]{2,1,0:T(1,128)S(1)}, f32[128,1,512]{2,1,0:T(1,128)}, u32[]{:S(2)}) %copy-start.1) | copy-done | bytes 262168
  4.2 0.0 copy-start.2
  4.2 0.8 %copy-done.2 = f32[32,512]{1,0:T(8,128)S(1)} copy-done((f32[32,512]{1,0:T(8,128)S(1)}, f32[32,512]{1,0:T(8,128)}, u32[]{:S(2)}) %copy-start.2) | copy-done | bytes 65560
  5.1 51.7 %shard_map.94 = (f32[2,16,256]{2,1,0:T(8,128)S(1)}, f32[16,512]{1,0:T(8,128)S(1)}, f32[8,128]{1,0:T(8,128)S(1)}) custom-call(bf16[2,16,256]{2,1,0:T(8,128)(2,1)S(1)} %bitcast.12, s32[1]{0:T(128)S(6)} %copy.14.length_ref, f32[128,1,512]{2,1,0:T(1,128)S(1)} %copy-done.1, f32[32,512]{1,0:T(8,128)S(1)} %copy-done.2, bf16[1024,512]{1,0:T(8,128)(2,1)S(1)} %bitcast.11, ...), custom_call_target="tpu_custom_call" | custom-call | tf_op jit(solution)/shard_map/pallas_call | solution.py:378
  56.8 0.6 %reshape.13 = f32[1,2,4096]{2,1,0:T(2,128)} reshape(f32[2,16,256]{2,1,0:T(8,128)S(1)} %get-tuple-element.6) | data formatting | bytes 65536 | tf_op jit(solution)/shard_map/reshape | solution.py:456
  57.4 0.6 slice_bitcast_fusion
  58.0 0.6 %copy.15 = f32[1,16,512]{2,1,0:T(8,128)} copy(f32[1,16,512]{2,1,0:T(8,128)S(1)} %bitcast.13) | data formatting | bytes 65536
Async XLA Ops:
  1.3 0.8 %copy-start.3 = (f32[1,512]{1,0:T(1,128)S(1)}, f32[1,512]{1,0:T(1,128)}, u32[]{:S(2)}) copy-start(f32[1,512]{1,0:T(1,128)} %bias.1) | copy-start | bytes 6148
  1.3 0.7 %copy-start.4 = (bf16[1,512]{1,0:T(2,128)(2,1)S(1)}, bf16[1,512]{1,0:T(2,128)(2,1)}, u32[]{:S(2)}) copy-start(bf16[1,512]{1,0:T(2,128)(2,1)} %head.1) | copy-start | bytes 3076
  2.0 1.2 %copy-start = (bf16[1,1024,512]{2,1,0:T(8,128)(2,1)S(1)}, bf16[1,1024,512]{2,1,0:T(8,128)(2,1)}, u32[]{:S(2)}) copy-start(bf16[1,1024,512]{2,1,0:T(8,128)(2,1)} %param.9) | copy-start | bytes 3145732
  3.3 0.9 %copy-start.1 = (f32[128,1,512]{2,1,0:T(1,128)S(1)}, f32[128,1,512]{2,1,0:T(1,128)}, u32[]{:S(2)}) copy-start(f32[128,1,512]{2,1,0:T(1,128)} %constant.4.clone.coarse_hbm) | copy-start | bytes 786436
  4.2 0.8 %copy-start.2 = (f32[32,512]{1,0:T(8,128)S(1)}, f32[32,512]{1,0:T(8,128)}, u32[]{:S(2)}) copy-start(f32[32,512]{1,0:T(8,128)} %constant.5.clone.fine_hbm) | copy-start | bytes 196612

commit v2 on v1

--- a/solution.py
+++ b/solution.py
@@ -28,6 +28,14 @@
     return coarse[:, None, :].astype(np.float32), fine.astype(np.float32)
 
 
+def cosine(angle):
+    square = angle * angle
+    total = jnp.full_like(square, 1.0 / math.factorial(16))
+    for power in range(14, -1, -2):
+        total = 1.0 / math.factorial(power) - total * square
+    return total
+
+
 def remote(src, dst, send_sem, recv_sem, device):
     return pltpu.make_async_remote_copy(
         src_ref=src,
@@ -40,16 +48,22 @@
 
 
 def kernel(
-    wave,
-    length_ref,
+    wave_hbm,
+    length_hbm,
     coarse_hbm,
     fine_hbm,
     weight_hbm,
-    bias,
-    head,
+    bias_hbm,
+    head_hbm,
     out_wave,
     out_first,
     out_head,
+    raw,
+    staged,
+    wave,
+    length_ref,
+    bias,
+    head,
     gathered,
     coarse,
     fine,
@@ -70,12 +84,12 @@
     pair_in,
     z_out,
     z_in,
+    z_own,
     heads,
     heads_mid,
     heads_all,
     core_heads,
     pair_heads,
-    zh_out,
     zh_in,
     wave_sum,
     wave_low,
@@ -95,6 +109,8 @@
     zh_recv,
     wave_send,
     wave_recv,
+    from_down,
+    from_up,
 ):
     clip = lax.axis_index("clip")
     disc = lax.axis_index("disc")
@@ -110,7 +126,6 @@
     frames = padded.shape[1] - 16
     shard = wave.shape[1]
     lanes = 128
-    steps = Z_SIZE // 2
 
     core_peer = {"clip": clip + 1 - 2 * core}
     pair_peer = {"clip": clip + 2 - 4 * y_lo}
@@ -121,17 +136,24 @@
     x_at = [lax.rem(x + k, X_SIZE) for k in range(X_SIZE)]
     x_peer = [{"disc": y_hi * X_SIZE + at} for at in x_at]
 
-    coarse_copy = pltpu.make_async_copy(coarse_hbm, coarse, local_sem.at[0])
-    fine_copy = pltpu.make_async_copy(fine_hbm, fine, local_sem.at[1])
-    weight_copy = pltpu.make_async_copy(weight_hbm, weight, local_sem.at[2])
+    local = ((wave_hbm, raw), (length_hbm, length_ref), (coarse_hbm, coarse), (fine_hbm, fine))
+    local += ((bias_hbm, bias), (head_hbm, head), (weight_hbm, weight))
+    copies = [
+        pltpu.make_async_copy(src, dst, local_sem.at[i]) for i, (src, dst) in enumerate(local)
+    ]
     barrier = pltpu.get_barrier_semaphore()
     peers = [y_peer, x_peer[2], x_peer[1], x_peer[3], z_up, z_down, pair_peer, core_peer]
     for peer in peers:
         pl.semaphore_signal(barrier, inc=1, device_id=peer, device_id_type=MESH)
-    coarse_copy.start()
-    fine_copy.start()
-    weight_copy.start()
-    gathered[disc] = wave[...]
+    for copy in copies:
+        copy.start()
+    copies[0].wait()
+    for h in range(shard):
+        part = raw[:, h * hop : (h + 1) * hop].astype(F32)
+        for ch in range(2):
+            staged[ch, h : h + 1, :] = part[ch : ch + 1, :]
+    wave[...] = staged[...].astype(BF16)
+    gathered[disc] = staged[...].astype(BF16)
     padded[:, 0:8, :] = jnp.zeros((2, 8, hop), F32)
     padded[:, frames + 8 : frames + 16, :] = jnp.zeros((2, 8, hop), F32)
     pl.semaphore_wait(barrier, len(peers))
@@ -144,8 +166,8 @@
     for copy in [to_y] + to_x:
         copy.start()
 
-    coarse_copy.wait()
-    fine_copy.wait()
+    for copy in copies[1:4]:
+        copy.wait()
     length = length_ref[0]
     start = lax.shift_right_arithmetic(frame - length, 1)
     length_float = length.astype(F32)
@@ -155,9 +177,9 @@
         row = pl.multiple_of(g * GROUP, GROUP)
         position = lax.broadcasted_iota(jnp.int32, (GROUP, lanes), 0) + (row - start)
         inside = (position >= 0) & (position < length)
-        phase = 2.0 * jnp.pi * position.astype(F32) / length_float
-        window = jnp.where(inside, 0.5 - 0.5 * jnp.cos(phase), 0.0)
-        factor = window * (1.0 / math.sqrt(frame))
+        angle = jnp.pi * position.astype(F32) / length_float - 0.5 * jnp.pi
+        root = cosine(angle)
+        factor = jnp.where(inside, root * root * (1.0 / math.sqrt(frame)), 0.0)
         for q in range(half // lanes):
             at = slice(q * lanes, (q + 1) * lanes)
             cos_a = coarse[g, :, at]
@@ -169,14 +191,27 @@
             table[pl.ds(row, GROUP), at] = real.astype(BF16)
             table[pl.ds(row, GROUP), half + q * lanes : half + (q + 1) * lanes] = imag.astype(BF16)
 
+    def relay():
+        pl.semaphore_signal(from_down, inc=1, device_id=z_up, device_id_type=MESH)
+        pl.semaphore_signal(from_up, inc=1, device_id=z_down, device_id_type=MESH)
+
+    def relay_wait():
+        pl.semaphore_wait(from_down, 1)
+        pl.semaphore_wait(from_up, 1)
+
+    relay()
     pl.loop(0, groups // 2)(table_rows)
     to_y.wait_recv()
     forward = [gather_copy(3 + k, gathered.at[other], other, x_peer[k]) for k in (2, 1, 3)]
     for copy in forward:
         copy.start()
+    relay_wait()
+    relay()
     pl.loop(groups // 2, groups)(table_rows)
     for copy in to_x + forward:
         copy.wait_recv()
+    relay_wait()
+    relay()
 
     for j in range(2 * X_SIZE):
         for ch in range(2):
@@ -189,7 +224,10 @@
     for n in range(4):
         at = slice(n * hop, (n + 1) * hop)
         spectrum[:, at] = jnp.dot(rows[...], table[:, at], preferred_element_type=F32).astype(BF16)
-    weight_copy.wait()
+    for copy in copies[4:]:
+        copy.wait()
+    relay_wait()
+    relay()
     preact[...] = jnp.dot(spectrum[...], weight[...], preferred_element_type=F32)
     head_wide = head[...].astype(F32)
     step = 32
@@ -222,13 +260,12 @@
         grad[n * 4 : (n + 1) * 4] = part
         grad_low[n * 4 : (n + 1) * 4] = part.astype(BF16)
 
-    def target(i):
-        s = i // 2
-        return lax.rem(z + Z_SIZE // 2 + s + lax.rem(i, 2) * (Z_SIZE - 1 - 2 * s), Z_SIZE)
+    relay_wait()
+    relay()
 
     def core_copy(i):
         return remote(
-            grad_low.at[target(i), :, 1 - core],
+            grad_low.at[i, :, 1 - core],
             core_in.at[i],
             core_send.at[i],
             core_recv.at[i],
@@ -263,6 +300,9 @@
         else:
             wave_sum[:, at, :] = wave_sum[:, at, :] + back
 
+    relay_wait()
+    relay()
+
     core_heads_copy.wait_recv()
     heads_mid[...] = heads[...] + core_heads[...]
     pair_heads_copy.start()
@@ -270,10 +310,12 @@
     @pl.loop(0, Z_SIZE)
     def _(i):
         core_copy(i).wait_recv()
-        at = target(i)
-        pair_out[i] = (grad[at, 1 - y_lo, core] + core_in[i, 1 - y_lo].astype(F32)).astype(BF16)
+        pair_out[i] = (grad[i, 1 - y_lo, core] + core_in[i, 1 - y_lo].astype(F32)).astype(BF16)
         pair_copy(i).start()
-        kept[i] = grad[at, y_lo, core] + core_in[i, y_lo].astype(F32)
+        kept[i] = grad[i, y_lo, core] + core_in[i, y_lo].astype(F32)
+
+    relay_wait()
+    relay()
 
     for j in range(2 * X_SIZE):
         for ch in range(2):
@@ -296,55 +338,64 @@
 
     pair_heads_copy.wait_recv()
     heads_all[...] = heads_mid[...] + pair_heads[...]
-
-    def z_copy(i, peer):
-        return remote(z_out.at[i], z_in.at[i], z_send.at[i], z_recv.at[i], peer)
-
-    def zh_copy(i, peer):
-        return remote(zh_out.at[i], zh_in.at[i], zh_send.at[i], zh_recv.at[i], peer)
-
-    for s in range(steps):
-        for up, peer in ((0, z_down), (1, z_up)):
-            i = 2 * s + up
-            pair_copy(i).wait_recv()
-            total = kept[i] + pair_in[i].astype(F32)
-            total_heads = heads_all[target(i) // 4]
-            if s > 0:
-                z_copy(i - 2, peer).wait_recv()
-                zh_copy(i - 2, peer).wait_recv()
-                total = total + z_in[i - 2].astype(F32)
-                total_heads = total_heads + zh_in[i - 2]
-            if i == Z_SIZE - 1:
-                last, last_heads = total, total_heads
-            else:
-                z_out[i] = total.astype(BF16)
-                z_copy(i, peer).start()
-                zh_out[i] = total_heads
-                zh_copy(i, peer).start()
-        if s == 1:
-            for k in (2, 1, 3):
-                x_copy(k).wait_recv()
-
-            def x_sum(at):
-                total = wave_low[at, x].astype(F32)
-                for k in range(3):
-                    total = total + x_in[k, at].astype(F32)
-                return total
-
-            y_out[...] = x_sum(1 - y_hi).astype(BF16)
-            y_copy.start()
-            out_wave[...] = x_sum(y_hi)
-        if s == 4:
-            y_copy.wait_recv()
-            out_wave[...] = out_wave[...] + y_in[...].astype(F32)
-
-    i = Z_SIZE - 2
-    z_copy(i, z_down).wait_recv()
-    zh_copy(i, z_down).wait_recv()
-    out_first[...] = last + z_in[i].astype(F32)
-    width = 2 * hidden_size // (4 * Z_SIZE * 2)
+    relay_wait()
+
+    def z_copy(to, slot):
+        peer = {"clip": to * 4 + inner}
+        return remote(z_out.at[to], z_in.at[slot], z_send.at[to], z_recv.at[slot], peer)
+
+    def zh_copy(to, slot):
+        peer = {"clip": to * 4 + inner}
+        return remote(heads_all.at[to // 4], zh_in.at[slot], zh_send.at[to], zh_recv.at[slot], peer)
+
+    @pl.loop(0, Z_SIZE)
+    def _(i):
+        pair_copy(i).wait_recv()
+        total = kept[i] + pair_in[i].astype(F32)
+
+        @pl.when(i != z)
+        def _():
+            z_out[i] = total.astype(BF16)
+            z_copy(i, z).start()
+            zh_copy(i, z).start()
+
+        @pl.when(i == z)
+        def _():
+            z_own[...] = total
+
+    for k in (2, 1, 3):
+        x_copy(k).wait_recv()
+
+    def x_sum(at):
+        total = wave_low[at, x].astype(F32)
+        for k in range(3):
+            total = total + x_in[k, at].astype(F32)
+        return total
+
+    y_out[...] = x_sum(1 - y_hi).astype(BF16)
+    y_copy.start()
+    out_wave[...] = x_sum(y_hi)
+    z_in[z] = jnp.zeros((GROUP, hidden_size), BF16)
+    zh_in[z] = heads_all[z // 4]
+    y_copy.wait_recv()
+    out_wave[...] = out_wave[...] + y_in[...].astype(F32)
+
+    @pl.loop(0, Z_SIZE)
+    def _(i):
+        @pl.when(i != z)
+        def _():
+            z_copy(i, i).wait_recv()
+            zh_copy(i, i).wait_recv()
+
+    total = z_own[...]
+    total_heads = zh_in[0]
+    for i in range(Z_SIZE):
+        total = total + z_in[i].astype(F32)
+        if i > 0:
+            total_heads = total_heads + zh_in[i]
+    out_first[...] = total
+    width = hidden_size // (4 * Z_SIZE)
     shift = lax.rem(lanes - width * lax.rem(clip, lanes // width), lanes)
-    total_heads = last_heads + zh_in[i]
     out_head[...] = pltpu.roll(jnp.concatenate([total_heads] * 4, axis=0), shift, axis=1)
 
     for copy in [to_y] + to_x + forward:
@@ -357,9 +408,13 @@
         core_copy(i).wait_send()
         pair_copy(i).wait_send()
 
-    for i in range(Z_SIZE - 1):
-        z_copy(i, z_up).wait_send()
-        zh_copy(i, z_up).wait_send()
+    @pl.loop(0, Z_SIZE)
+    def _(i):
+        @pl.when(i != z)
+        def _():
+            z_copy(i, z).wait_send()
+            zh_copy(i, z).wait_send()
+
     for k in (2, 1, 3):
         x_copy(k).wait_send()
     y_copy.wait_send()
@@ -373,7 +428,7 @@
     count = 2 * frames
     block = (GROUP, hidden_size)
     vmem = pl.BlockSpec(memory_space=pltpu.VMEM)
-    any_space = pl.BlockSpec(memory_space=pl.ANY)
+    hbm = pl.BlockSpec(memory_space=pltpu.HBM)
     coarse, fine = [jnp.asarray(part) for part in twiddles(frame)]
     out_wave, out_first, out_head = pl.pallas_call(
         kernel,
@@ -382,17 +437,15 @@
             jax.ShapeDtypeStruct(block, F32),
             jax.ShapeDtypeStruct((8, 128), F32),
         ),
-        in_specs=[
-            vmem,
-            pl.BlockSpec(memory_space=pltpu.SMEM),
-            any_space,
-            any_space,
-            any_space,
-            vmem,
-            vmem,
-        ],
+        in_specs=[hbm] * 7,
         out_specs=(vmem, vmem, vmem),
         scratch_shapes=[
+            pltpu.VMEM((2, shard * hop), BF16),
+            pltpu.VMEM((2, shard, hop), F32),
+            pltpu.VMEM((2, shard, hop), BF16),
+            pltpu.SMEM((1,), jnp.int32),
+            pltpu.VMEM((1, hidden_size), F32),
+            pltpu.VMEM((1, hidden_size), BF16),
             pltpu.VMEM((2 * X_SIZE, 2, shard, hop), BF16),
             pltpu.VMEM(coarse.shape, F32),
             pltpu.VMEM(fine.shape, F32),
@@ -413,19 +466,19 @@
             pltpu.VMEM((Z_SIZE,) + block, BF16),
             pltpu.VMEM((Z_SIZE,) + block, BF16),
             pltpu.VMEM((Z_SIZE,) + block, BF16),
+            pltpu.VMEM(block, F32),
             pltpu.VMEM((hidden_size // 128, 2, 128), F32),
             pltpu.VMEM((hidden_size // 128, 2, 128), F32),
             pltpu.VMEM((hidden_size // 128, 2, 128), F32),
             pltpu.VMEM((hidden_size // 128, 2, 128), F32),
             pltpu.VMEM((hidden_size // 128, 2, 128), F32),
             pltpu.VMEM((Z_SIZE, 2, 128), F32),
-            pltpu.VMEM((Z_SIZE, 2, 128), F32),
             pltpu.VMEM((2, frames + 16, hop), F32),
             pltpu.VMEM((2, X_SIZE, 2, shard, hop), BF16),
             pltpu.VMEM((3, 2, 2, shard, hop), BF16),
             pltpu.VMEM((2, shard, hop), BF16),
             pltpu.VMEM((2, shard, hop), BF16),
-            pltpu.SemaphoreType.DMA((3,)),
+            pltpu.SemaphoreType.DMA((7,)),
             pltpu.SemaphoreType.DMA((7,)),
             pltpu.SemaphoreType.DMA((7,)),
             pltpu.SemaphoreType.DMA((Z_SIZE + 1,)),
@@ -438,12 +491,14 @@
             pltpu.SemaphoreType.DMA((Z_SIZE,)),
             pltpu.SemaphoreType.DMA((4,)),
             pltpu.SemaphoreType.DMA((4,)),
+            pltpu.SemaphoreType.REGULAR,
+            pltpu.SemaphoreType.REGULAR,
         ],
         compiler_params=pltpu.CompilerParams(
             collective_id=0, has_side_effects=True, vmem_limit_bytes=48 * 1024 * 1024
         ),
     )(
-        waveform.reshape(2, shard, hop),
+        waveform[0],
         window_length,
         coarse,
         fine,

time: 58.9 us -> 48.4 us (0.82)
  the two profiles are of different devices: /device:TPU:16 before, /device:TPU:96 now
where the time goes in v2:
time: 48.4 us; the launch traced here: 48 us
  Pallas kernels  40.5 us (84%)
  local copies, waits for them, and re-layouts  6.22 us (13%)
  between operations  1.32 us (3%)
    pallas_call x1, Pallas kernels, body(): pl.pallas_call(kernel, out_shape=(jax.ShapeDtypeStruct((2, shard, hop), F...  40.5 us
    unnamed x13, local copies, waits for them, and re-layouts  5.02 us

profile of v2, /device:TPU:96, one launch (start us, length us, event | category | flops | bytes accessed | tf_op | source)
XLA Modules:
  0.0 48.0 jit_solution(2440568994496592117)
XLA Ops:
  0.6 0.0 copy-start.5
  1.3 0.0 copy-start.4
  1.3 0.0 copy-done.5
  1.3 0.7 %copy-done.4 = f32[1,512]{1,0:T(1,128)S(1)} copy-done((f32[1,512]{1,0:T(1,128)S(1)}, f32[1,512]{1,0:T(1,128)}, u32[]{:S(2)}) %copy-start.4) | copy-done | bytes 2072
  2.0 0.0 copy-start
  2.0 1.2 %copy-done = bf16[1,1024,512]{2,1,0:T(8,128)(2,1)S(1)} copy-done((bf16[1,1024,512]{2,1,0:T(8,128)(2,1)S(1)}, bf16[1,1024,512]{2,1,0:T(8,128)(2,1)}, u32[]{:S(2)}) %copy-start) | copy-done | bytes 1048600
  3.2 0.0 copy-start.1
  3.2 0.9 %copy-done.1 = f32[128,1,512]{2,1,0:T(1,128)S(1)} copy-done((f32[128,1,512]{2,1,0:T(1,128)S(1)}, f32[128,1,512]{2,1,0:T(1,128)}, u32[]{:S(2)}) %copy-start.1) | copy-done | bytes 262168
  4.2 0.0 copy-start.2
  4.2 0.8 %copy-done.2 = f32[32,512]{1,0:T(8,128)S(1)} copy-done((f32[32,512]{1,0:T(8,128)S(1)}, f32[32,512]{1,0:T(8,128)}, u32[]{:S(2)}) %copy-start.2) | copy-done | bytes 65560
  5.0 0.0 copy-start.3
  5.0 0.7 %copy-done.3 = bf16[1,2,4096]{2,1,0:T(2,128)(2,1)S(1)} copy-done((bf16[1,2,4096]{2,1,0:T(2,128)(2,1)S(1)}, bf16[1,2,4096]{2,1,0:T(2,128)(2,1)}, u32[]{:S(2)}) %copy-start.3) | copy-done | bytes 16408
  5.7 40.5 %shard_map.94 = (f32[2,16,256]{2,1,0:T(8,128)S(1)}, f32[16,512]{1,0:T(8,128)S(1)}, f32[8,128]{1,0:T(8,128)S(1)}) custom-call(bf16[2,4096]{1,0:T(2,128)(2,1)S(1)} %bitcast.9, s32[1]{0:T(128)S(6)} %copy.11.length_hbm, f32[128,1,512]{2,1,0:T(1,128)S(1)} %copy-done.1, f32[32,512]{1,0:T(8,128)S(1)} %copy-done.2, bf16[1024,512]{1,0:T(8,128)(2,1)S(1)} %bitcast.7, ...), custom_call_target="tpu_custom_call" | custom-call | tf_op jit(solution)/shard_map/pallas_call | solution.py:433
  46.2 0.6 %reshape.9 = f32[1,2,4096]{2,1,0:T(2,128)} reshape(f32[2,16,256]{2,1,0:T(8,128)S(1)} %get-tuple-element.6) | data formatting | bytes 65536 | tf_op jit(solution)/shard_map/reshape | solution.py:511
  46.9 0.6 %slice_bitcast_fusion = f32[1,8,2]{1,2,0:T(2,128)} fusion(f32[8,128]{1,0:T(8,128)S(1)} %get-tuple-element.8), kind=kLoop, calls=%fused_computation | loop fusion | bytes 128 | tf_op jit(solution)/shard_map/broadcast_in_dim | solution.py:513
  47.4 0.6 %copy.12 = f32[1,16,512]{2,1,0:T(8,128)} copy(f32[1,16,512]{2,1,0:T(8,128)S(1)} %bitcast.8) | data formatting | bytes 65536
Async XLA Ops:
  0.6 0.7 %copy-start.5 = (bf16[1,512]{1,0:T(2,128)(2,1)S(1)}, bf16[1,512]{1,0:T(2,128)(2,1)}, u32[]{:S(2)}) copy-start(bf16[1,512]{1,0:T(2,128)(2,1)} %head_hbm.1) | copy-start | bytes 3076
  1.3 0.7 %copy-start.4 = (f32[1,512]{1,0:T(1,128)S(1)}, f32[1,512]{1,0:T(1,128)}, u32[]{:S(2)}) copy-start(f32[1,512]{1,0:T(1,128)} %bias_hbm.1) | copy-start | bytes 6148
  2.0 1.2 %copy-start = (bf16[1,1024,512]{2,1,0:T(8,128)(2,1)S(1)}, bf16[1,1024,512]{2,1,0:T(8,128)(2,1)}, u32[]{:S(2)}) copy-start(bf16[1,1024,512]{2,1,0:T(8,128)(2,1)} %param.9) | copy-start | bytes 3145732
  3.2 0.9 %copy-start.1 = (f32[128,1,512]{2,1,0:T(1,128)S(1)}, f32[128,1,512]{2,1,0:T(1,128)}, u32[]{:S(2)}) copy-start(f32[128,1,512]{2,1,0:T(1,128)} %constant.4.clone.coarse_hbm) | copy-start | bytes 786436
  4.2 0.8 %copy-start.2 = (f32[32,512]{1,0:T(8,128)S(1)}, f32[32,512]{1,0:T(8,128)}, u32[]{:S(2)}) copy-start(f32[32,512]{1,0:T(8,128)} %constant.5.clone.fine_hbm) | copy-start | bytes 196612
  5.0 0.7 %copy-start.3 = (bf16[1,2,4096]{2,1,0:T(2,128)(2,1)S(1)}, bf16[1,2,4096]{2,1,0:T(2,128)(2,1)}, u32[]{:S(2)}) copy-start(bf16[1,2,4096]{2,1,0:T(2,128)(2,1)} %param.7) | copy-start | bytes 49156

commit v3 on v2

--- a/solution.py
+++ b/solution.py
@@ -48,8 +48,8 @@
 
 
 def kernel(
+    length_ref,
     wave_hbm,
-    length_hbm,
     coarse_hbm,
     fine_hbm,
     weight_hbm,
@@ -61,7 +61,6 @@
     raw,
     staged,
     wave,
-    length_ref,
     bias,
     head,
     gathered,
@@ -109,8 +108,7 @@
     zh_recv,
     wave_send,
     wave_recv,
-    from_down,
-    from_up,
+    near_sem,
 ):
     clip = lax.axis_index("clip")
     disc = lax.axis_index("disc")
@@ -129,20 +127,21 @@
 
     core_peer = {"clip": clip + 1 - 2 * core}
     pair_peer = {"clip": clip + 2 - 4 * y_lo}
-    z_up = {"clip": lax.rem(z + 1, Z_SIZE) * 4 + inner}
-    z_down = {"clip": lax.rem(z + Z_SIZE - 1, Z_SIZE) * 4 + inner}
+    z_near = [
+        {"clip": lax.rem(z + away, Z_SIZE) * 4 + inner} for away in (1, 2, Z_SIZE - 1, Z_SIZE - 2)
+    ]
     other = lax.rem(disc + X_SIZE, 2 * X_SIZE)
     y_peer = {"disc": other}
     x_at = [lax.rem(x + k, X_SIZE) for k in range(X_SIZE)]
     x_peer = [{"disc": y_hi * X_SIZE + at} for at in x_at]
 
-    local = ((wave_hbm, raw), (length_hbm, length_ref), (coarse_hbm, coarse), (fine_hbm, fine))
+    local = ((wave_hbm, raw), (coarse_hbm, coarse), (fine_hbm, fine))
     local += ((bias_hbm, bias), (head_hbm, head), (weight_hbm, weight))
     copies = [
         pltpu.make_async_copy(src, dst, local_sem.at[i]) for i, (src, dst) in enumerate(local)
     ]
     barrier = pltpu.get_barrier_semaphore()
-    peers = [y_peer, x_peer[2], x_peer[1], x_peer[3], z_up, z_down, pair_peer, core_peer]
+    peers = [y_peer, x_peer[2], x_peer[1], x_peer[3], *z_near, pair_peer, core_peer]
     for peer in peers:
         pl.semaphore_signal(barrier, inc=1, device_id=peer, device_id_type=MESH)
     for copy in copies:
@@ -166,7 +165,7 @@
     for copy in [to_y] + to_x:
         copy.start()
 
-    for copy in copies[1:4]:
+    for copy in copies[1:3]:
         copy.wait()
     length = length_ref[0]
     start = lax.shift_right_arithmetic(frame - length, 1)
@@ -191,28 +190,22 @@
             table[pl.ds(row, GROUP), at] = real.astype(BF16)
             table[pl.ds(row, GROUP), half + q * lanes : half + (q + 1) * lanes] = imag.astype(BF16)
 
-    def relay():
-        pl.semaphore_signal(from_down, inc=1, device_id=z_up, device_id_type=MESH)
-        pl.semaphore_signal(from_up, inc=1, device_id=z_down, device_id_type=MESH)
-
-    def relay_wait():
-        pl.semaphore_wait(from_down, 1)
-        pl.semaphore_wait(from_up, 1)
-
-    relay()
+    def relay(turn):
+        for peer in z_near:
+            pl.semaphore_signal(near_sem.at[turn], inc=1, device_id=peer, device_id_type=MESH)
+
+    def relay_wait(turn):
+        pl.semaphore_wait(near_sem.at[turn], len(z_near))
+
+    relay(0)
     pl.loop(0, groups // 2)(table_rows)
     to_y.wait_recv()
     forward = [gather_copy(3 + k, gathered.at[other], other, x_peer[k]) for k in (2, 1, 3)]
     for copy in forward:
         copy.start()
-    relay_wait()
-    relay()
     pl.loop(groups // 2, groups)(table_rows)
     for copy in to_x + forward:
         copy.wait_recv()
-    relay_wait()
-    relay()
-
     for j in range(2 * X_SIZE):
         for ch in range(2):
             padded[ch, 8 + shard * j : 8 + shard * (j + 1), :] = gathered[j, ch].astype(F32)
@@ -224,10 +217,8 @@
     for n in range(4):
         at = slice(n * hop, (n + 1) * hop)
         spectrum[:, at] = jnp.dot(rows[...], table[:, at], preferred_element_type=F32).astype(BF16)
-    for copy in copies[4:]:
+    for copy in copies[3:]:
         copy.wait()
-    relay_wait()
-    relay()
     preact[...] = jnp.dot(spectrum[...], weight[...], preferred_element_type=F32)
     head_wide = head[...].astype(F32)
     step = 32
@@ -260,9 +251,6 @@
         grad[n * 4 : (n + 1) * 4] = part
         grad_low[n * 4 : (n + 1) * 4] = part.astype(BF16)
 
-    relay_wait()
-    relay()
-
     def core_copy(i):
         return remote(
             grad_low.at[i, :, 1 - core],
@@ -283,6 +271,9 @@
     )
     core_heads_copy.start()
     pl.loop(0, Z_SIZE)(lambda i: core_copy(i).start())
+
+    relay_wait(0)
+    relay(1)
 
     spec_delta[...] = lax.dot_general(
         gen_delta[...], weight[...], (((1,), (1,)), ((), ())), preferred_element_type=F32
@@ -300,8 +291,8 @@
         else:
             wave_sum[:, at, :] = wave_sum[:, at, :] + back
 
-    relay_wait()
-    relay()
+    relay_wait(1)
+    relay(2)
 
     core_heads_copy.wait_recv()
     heads_mid[...] = heads[...] + core_heads[...]
@@ -313,9 +304,6 @@
         pair_out[i] = (grad[i, 1 - y_lo, core] + core_in[i, 1 - y_lo].astype(F32)).astype(BF16)
         pair_copy(i).start()
         kept[i] = grad[i, y_lo, core] + core_in[i, y_lo].astype(F32)
-
-    relay_wait()
-    relay()
 
     for j in range(2 * X_SIZE):
         for ch in range(2):
@@ -338,7 +326,7 @@
 
     pair_heads_copy.wait_recv()
     heads_all[...] = heads_mid[...] + pair_heads[...]
-    relay_wait()
+    relay_wait(2)
 
     def z_copy(to, slot):
         peer = {"clip": to * 4 + inner}
@@ -430,6 +418,7 @@
     vmem = pl.BlockSpec(memory_space=pltpu.VMEM)
     hbm = pl.BlockSpec(memory_space=pltpu.HBM)
     coarse, fine = [jnp.asarray(part) for part in twiddles(frame)]
+    operands = (waveform[0], coarse, fine, first_weight[0], first_bias, head_weight)
     out_wave, out_first, out_head = pl.pallas_call(
         kernel,
         out_shape=(
@@ -437,13 +426,12 @@
             jax.ShapeDtypeStruct(block, F32),
             jax.ShapeDtypeStruct((8, 128), F32),
         ),
-        in_specs=[hbm] * 7,
+        in_specs=[pl.BlockSpec(memory_space=pltpu.SMEM)] + [hbm] * len(operands),
         out_specs=(vmem, vmem, vmem),
         scratch_shapes=[
             pltpu.VMEM((2, shard * hop), BF16),
             pltpu.VMEM((2, shard, hop), F32),
             pltpu.VMEM((2, shard, hop), BF16),
-            pltpu.SMEM((1,), jnp.int32),
             pltpu.VMEM((1, hidden_size), F32),
             pltpu.VMEM((1, hidden_size), BF16),
             pltpu.VMEM((2 * X_SIZE, 2, shard, hop), BF16),
@@ -478,7 +466,7 @@
             pltpu.VMEM((3, 2, 2, shard, hop), BF16),
             pltpu.VMEM((2, shard, hop), BF16),
             pltpu.VMEM((2, shard, hop), BF16),
-            pltpu.SemaphoreType.DMA((7,)),
+            pltpu.SemaphoreType.DMA((6,)),
             pltpu.SemaphoreType.DMA((7,)),
             pltpu.SemaphoreType.DMA((7,)),
             pltpu.SemaphoreType.DMA((Z_SIZE + 1,)),
@@ -491,21 +479,12 @@
             pltpu.SemaphoreType.DMA((Z_SIZE,)),
             pltpu.SemaphoreType.DMA((4,)),
             pltpu.SemaphoreType.DMA((4,)),
-            pltpu.SemaphoreType.REGULAR,
-            pltpu.SemaphoreType.REGULAR,
+            pltpu.SemaphoreType.REGULAR((3,)),
         ],
         compiler_params=pltpu.CompilerParams(
-            collective_id=0, has_side_effects=True, vmem_limit_bytes=48 * 1024 * 1024
+            collective_id=0, has_side_effects=True, vmem_limit_bytes=53000 * 1024
         ),
-    )(
-        waveform[0],
-        window_length,
-        coarse,
-        fine,
-        first_weight[0],
-        first_bias,
-        head_weight,
-    )
+    )(window_length, *[pltpu.with_memory_space_constraint(part, pltpu.HBM) for part in operands])
     width = 8
     return (
         out_wave.reshape(1, 2, shard * hop),

time: 48.4 us -> 43.7 us (0.903)
  the two profiles are of different devices: /device:TPU:96 before, /device:TPU:8 now
where the time goes in v3:
time: 43.7 us; the launch traced here: 43.5 us
  Pallas kernels  40.4 us (92%)
  local copies, waits for them, and re-layouts  1.82 us (4%)
  between operations  1.29 us (3%)
    pallas_call x1, Pallas kernels, body(): pl.pallas_call(kernel, out_shape=(jax.ShapeDtypeStruct((2, shard, hop), F...  40.4 us

profile of v3, /device:TPU:8, one launch (start us, length us, event | category | flops | bytes accessed | tf_op | source)
XLA Modules:
  0.0 43.5 jit_solution(18416707952175490822)
XLA Ops:
  1.3 40.4 %shard_map.94 = (f32[2,16,256]{2,1,0:T(8,128)S(1)}, f32[16,512]{1,0:T(8,128)S(1)}, f32[8,128]{1,0:T(8,128)S(1)}) custom-call(s32[1]{0:T(128)S(6)} %copy.11.length_ref, bf16[2,4096]{1,0:T(2,128)(2,1)} %bitcast.9, f32[128,1,512]{2,1,0:T(1,128)} %constant.4.clone.coarse_hbm, f32[32,512]{1,0:T(8,128)} %constant.5.clone.fine_hbm, bf16[1024,512]{1,0:T(8,128)(2,1)} %bitcast.8, ...), custom_call_target="tpu_custom_call" | custom-call | tf_op jit(solution)/shard_map/pallas_call | solution.py:422
  41.7 0.6 %reshape.9 = f32[1,2,4096]{2,1,0:T(2,128)} reshape(f32[2,16,256]{2,1,0:T(8,128)S(1)} %get-tuple-element.6) | data formatting | bytes 65536 | tf_op jit(solution)/shard_map/reshape | solution.py:490
  42.3 0.6 %slice_bitcast_fusion = f32[1,8,2]{1,2,0:T(2,128)} fusion(f32[8,128]{1,0:T(8,128)S(1)} %get-tuple-element.8), kind=kLoop, calls=%fused_computation | loop fusion | bytes 128 | tf_op jit(solution)/shard_map/broadcast_in_dim | solution.py:492
  42.9 0.6 %copy.12 = f32[1,16,512]{2,1,0:T(8,128)} copy(f32[1,16,512]{2,1,0:T(8,128)S(1)} %bitcast.7) | data formatting | bytes 65536

commit v4 on v3

--- a/solution.py
+++ b/solution.py
@@ -142,9 +142,10 @@
     ]
     barrier = pltpu.get_barrier_semaphore()
     peers = [y_peer, x_peer[2], x_peer[1], x_peer[3], *z_near, pair_peer, core_peer]
+    copies[0].start()
     for peer in peers:
         pl.semaphore_signal(barrier, inc=1, device_id=peer, device_id_type=MESH)
-    for copy in copies:
+    for copy in copies[1:]:
         copy.start()
     copies[0].wait()
     for h in range(shard):
@@ -362,11 +363,35 @@
 
     y_out[...] = x_sum(1 - y_hi).astype(BF16)
     y_copy.start()
-    out_wave[...] = x_sum(y_hi)
+    staged[...] = x_sum(y_hi)
     z_in[z] = jnp.zeros((GROUP, hidden_size), BF16)
     zh_in[z] = heads_all[z // 4]
     y_copy.wait_recv()
-    out_wave[...] = out_wave[...] + y_in[...].astype(F32)
+    staged[...] = staged[...] + y_in[...].astype(F32)
+    for h in range(shard):
+        for ch in range(2):
+            out_wave[ch : ch + 1, h * hop : (h + 1) * hop] = staged[ch, h : h + 1, :]
+
+    for copy in [to_y] + to_x + forward:
+        copy.wait_send()
+    core_heads_copy.wait_send()
+    pair_heads_copy.wait_send()
+
+    @pl.loop(0, Z_SIZE)
+    def _(i):
+        core_copy(i).wait_send()
+        pair_copy(i).wait_send()
+
+    @pl.loop(0, Z_SIZE)
+    def _(i):
+        @pl.when(i != z)
+        def _():
+            z_copy(i, z).wait_send()
+            zh_copy(i, z).wait_send()
+
+    for k in (2, 1, 3):
+        x_copy(k).wait_send()
+    y_copy.wait_send()
 
     @pl.loop(0, Z_SIZE)
     def _(i):
@@ -384,28 +409,17 @@
     out_first[...] = total
     width = hidden_size // (4 * Z_SIZE)
     shift = lax.rem(lanes - width * lax.rem(clip, lanes // width), lanes)
-    out_head[...] = pltpu.roll(jnp.concatenate([total_heads] * 4, axis=0), shift, axis=1)
-
-    for copy in [to_y] + to_x + forward:
-        copy.wait_send()
-    core_heads_copy.wait_send()
-    pair_heads_copy.wait_send()
-
-    @pl.loop(0, Z_SIZE)
-    def _(i):
-        core_copy(i).wait_send()
-        pair_copy(i).wait_send()
-
-    @pl.loop(0, Z_SIZE)
-    def _(i):
-        @pl.when(i != z)
-        def _():
-            z_copy(i, z).wait_send()
-            zh_copy(i, z).wait_send()
-
-    for k in (2, 1, 3):
-        x_copy(k).wait_send()
-    y_copy.wait_send()
+    rolled = pltpu.roll(jnp.concatenate([total_heads] * 4, axis=0), shift, axis=1)
+    out_head[...] = rolled[0:2, 0:width]
+
+
+def store(*refs):
+    sem = refs[6]
+    copies = [pltpu.make_async_copy(refs[i], refs[3 + i], sem.at[i]) for i in range(3)]
+    for copy in copies:
+        copy.start()
+    for copy in copies:
+        copy.wait()
 
 
 def body(waveform, window_length, first_weight, first_bias, head_weight):
@@ -419,13 +433,14 @@
     hbm = pl.BlockSpec(memory_space=pltpu.HBM)
     coarse, fine = [jnp.asarray(part) for part in twiddles(frame)]
     operands = (waveform[0], coarse, fine, first_weight[0], first_bias, head_weight)
-    out_wave, out_first, out_head = pl.pallas_call(
+    results = (
+        jax.ShapeDtypeStruct((2, shard * hop), F32),
+        jax.ShapeDtypeStruct(block, F32),
+        jax.ShapeDtypeStruct((2, hidden_size // (4 * Z_SIZE)), F32),
+    )
+    outs = pl.pallas_call(
         kernel,
-        out_shape=(
-            jax.ShapeDtypeStruct((2, shard, hop), F32),
-            jax.ShapeDtypeStruct(block, F32),
-            jax.ShapeDtypeStruct((8, 128), F32),
-        ),
+        out_shape=results,
         in_specs=[pl.BlockSpec(memory_space=pltpu.SMEM)] + [hbm] * len(operands),
         out_specs=(vmem, vmem, vmem),
         scratch_shapes=[
@@ -485,12 +500,15 @@
             collective_id=0, has_side_effects=True, vmem_limit_bytes=53000 * 1024
         ),
     )(window_length, *[pltpu.with_memory_space_constraint(part, pltpu.HBM) for part in operands])
-    width = 8
-    return (
-        out_wave.reshape(1, 2, shard * hop),
-        out_first[None],
-        out_head[:2, :width].T[None],
-    )
+    out_wave, out_first, out_head = pl.pallas_call(
+        store,
+        out_shape=results,
+        in_specs=[vmem] * 3,
+        out_specs=[hbm] * 3,
+        scratch_shapes=[pltpu.SemaphoreType.DMA((3,))],
+        compiler_params=pltpu.CompilerParams(vmem_limit_bytes=1024 * 1024),
+    )(*outs)
+    return out_wave[None], out_first[None], out_head.T[None]
 
 
 def solution(mesh):

time: 43.7 us -> 42.8 us (0.979)
  local copies, waits for them, and re-layouts: 1.82 us -> 0 us
  Pallas kernels: 40.4 us -> 41.3 us
    pallas_call x1 -> x2, Pallas kernels: 40.4 us -> 41.3 us  [the longest x1 40.7 us: body(): pl.pallas_call(kernel, out_shape=results, in_specs=[pl.BlockSpec(memory_s...]
    reshape x1 -> x0, local copies, waits for them, and re-layouts: 0.64 us -> none  [body(): out_wave.reshape(1, 2, shard * hop)]
    unnamed x1 -> x0, local copies, waits for them, and re-layouts: 0.61 us -> none
    broadcast_in_dim x1 -> x0, local copies, waits for them, and re-layouts: 0.56 us -> none  [body(): out_head[:2, :width].T[None]]
where the time goes in v4:
time: 42.8 us; the launch traced here: 42.6 us
  Pallas kernels  41.3 us (96%)
  between operations  1.28 us (3%)
    pallas_call x1, Pallas kernels, body(): pl.pallas_call(kernel, out_shape=results, in_specs=[pl.BlockSpec(memory_s...  40.7 us

profile of v4, /device:TPU:8, one launch (start us, length us, event | category | flops | bytes accessed | tf_op | source)
XLA Modules:
  0.0 42.6 jit_solution(13728089957817113501)
XLA Ops:
  1.3 40.7 %shard_map.94 = (f32[2,4096]{1,0:T(2,128)S(1)}, f32[16,512]{1,0:T(8,128)S(1)}, f32[2,8]{1,0:T(2,128)S(1)}) custom-call(s32[1]{0:T(128)S(6)} %copy.10.length_ref, bf16[2,4096]{1,0:T(2,128)(2,1)} %bitcast.8, f32[128,1,512]{2,1,0:T(1,128)} %constant.4.clone.coarse_hbm, f32[32,512]{1,0:T(8,128)} %constant.5.clone.fine_hbm, bf16[1024,512]{1,0:T(8,128)(2,1)} %bitcast.7, ...), custom_call_target="tpu_custom_call" | custom-call | tf_op jit(solution)/shard_map/pallas_call | solution.py:441
  41.9 0.7 %shard_map.95 = (f32[2,4096]{1,0:T(2,128)}, f32[16,512]{1,0:T(8,128)}, f32[2,8]{1,0:T(2,128)}) custom-call(f32[2,4096]{1,0:T(2,128)S(1)} %get-tuple-element.9.refs_0_, f32[16,512]{1,0:T(8,128)S(1)} %get-tuple-element.10.refs_1_, f32[2,8]{1,0:T(2,128)S(1)} %get-tuple-element.11.refs_2_), custom_call_target="tpu_custom_call" | custom-call | tf_op jit(solution)/shard_map/pallas_call | solution.py:503

commit v5 on v4

--- a/solution.py
+++ b/solution.py
@@ -222,7 +222,7 @@
         copy.wait()
     preact[...] = jnp.dot(spectrum[...], weight[...], preferred_element_type=F32)
     head_wide = head[...].astype(F32)
-    step = 32
+    step = 64
 
     def delta_rows(i, sums):
         at = pl.ds(pl.multiple_of(i * step, step), step)
@@ -239,18 +239,10 @@
         )
 
     zero = jnp.zeros((1, hidden_size), F32)
-    sums = lax.fori_loop(0, 2 * frames // step, delta_rows, (zero, zero))
+    sums = lax.fori_loop(0, 2 * frames // step, delta_rows, (zero, zero), unroll=2)
     for r in range(hidden_size // lanes):
         for t in range(2):
             heads[r, t : t + 1, :] = sums[t][:, r * lanes : (r + 1) * lanes]
-
-    for n in range(4):
-        at = slice(n * hop, (n + 1) * hop)
-        part = lax.dot_general(
-            spectrum[:, at], disc_delta[...], (((0,), (0,)), ((), ())), preferred_element_type=F32
-        ).reshape(Z_SIZE // 4, 2, 2, GROUP, hidden_size)
-        grad[n * 4 : (n + 1) * 4] = part
-        grad_low[n * 4 : (n + 1) * 4] = part.astype(BF16)
 
     def core_copy(i):
         return remote(
@@ -271,7 +263,16 @@
         heads_mid, pair_heads, pair_send.at[Z_SIZE], pair_recv.at[Z_SIZE], pair_peer
     )
     core_heads_copy.start()
-    pl.loop(0, Z_SIZE)(lambda i: core_copy(i).start())
+    for n in range(4):
+        at = slice(n * hop, (n + 1) * hop)
+        part = lax.dot_general(
+            spectrum[:, at], disc_delta[...], (((0,), (0,)), ((), ())), preferred_element_type=F32
+        ).reshape(Z_SIZE // 4, 2, 2, GROUP, hidden_size)
+        grad[n * 4 : (n + 1) * 4] = part
+        grad_low[n * 4 : (n + 1) * 4] = part.astype(BF16)
+        if n > 0:
+            pl.loop(4 * (n - 1), 4 * n)(lambda i: core_copy(i).start())
+    pl.loop(Z_SIZE - 4, Z_SIZE)(lambda i: core_copy(i).start())
 
     relay_wait(0)
     relay(1)

time: 42.8 us -> 41.4 us (0.967)
  Pallas kernels: 41.3 us -> 40 us
    pallas_call x1, Pallas kernels: 40.7 us -> 39.3 us  [body(): pl.pallas_call(kernel, out_shape=results, in_specs=[pl.BlockSpec(memory_s...]
where the time goes in v5:
time: 41.4 us; the launch traced here: 41.2 us
  Pallas kernels  40 us (97%)
  between operations  1.28 us (3%)
    pallas_call x1, Pallas kernels, body(): pl.pallas_call(kernel, out_shape=results, in_specs=[pl.BlockSpec(memory_s...  39.3 us

profile of v5, /device:TPU:8, one launch (start us, length us, event | category | flops | bytes accessed | tf_op | source)
XLA Modules:
  0.0 41.2 jit_solution(8459981586323398842)
XLA Ops:
  1.3 39.3 %shard_map.94 = (f32[2,4096]{1,0:T(2,128)S(1)}, f32[16,512]{1,0:T(8,128)S(1)}, f32[2,8]{1,0:T(2,128)S(1)}) custom-call(s32[1]{0:T(128)S(6)} %copy.10.length_ref, bf16[2,4096]{1,0:T(2,128)(2,1)} %bitcast.8, f32[128,1,512]{2,1,0:T(1,128)} %constant.4.clone.coarse_hbm, f32[32,512]{1,0:T(8,128)} %constant.5.clone.fine_hbm, bf16[1024,512]{1,0:T(8,128)(2,1)} %bitcast.7, ...), custom_call_target="tpu_custom_call" | custom-call | tf_op jit(solution)/shard_map/pallas_call | solution.py:442
  40.6 0.7 %shard_map.95 = (f32[2,4096]{1,0:T(2,128)}, f32[16,512]{1,0:T(8,128)}, f32[2,8]{1,0:T(2,128)}) custom-call(f32[2,4096]{1,0:T(2,128)S(1)} %get-tuple-element.9.refs_0_, f32[16,512]{1,0:T(8,128)S(1)} %get-tuple-element.10.refs_1_, f32[2,8]{1,0:T(2,128)S(1)} %get-tuple-element.11.refs_2_), custom_call_target="tpu_custom_call" | custom-call | tf_op jit(solution)/shard_map/pallas_call | solution.py:504

commit v6 on v5

--- a/solution.py
+++ b/solution.py
@@ -239,7 +239,7 @@
         )
 
     zero = jnp.zeros((1, hidden_size), F32)
-    sums = lax.fori_loop(0, 2 * frames // step, delta_rows, (zero, zero), unroll=2)
+    sums = lax.fori_loop(0, 2 * frames // step, delta_rows, (zero, zero), unroll=4)
     for r in range(hidden_size // lanes):
         for t in range(2):
             heads[r, t : t + 1, :] = sums[t][:, r * lanes : (r + 1) * lanes]
@@ -300,7 +300,7 @@
     heads_mid[...] = heads[...] + core_heads[...]
     pair_heads_copy.start()
 
-    @pl.loop(0, Z_SIZE)
+    @pl.loop(0, Z_SIZE, unroll=2)
     def _(i):
         core_copy(i).wait_recv()
         pair_out[i] = (grad[i, 1 - y_lo, core] + core_in[i, 1 - y_lo].astype(F32)).astype(BF16)

time: 41.4 us -> 41.3 us (level)
  no operation moved by 1% of the time
where the time goes in v6:
time: 41.3 us; the launch traced here: 41.1 us
  Pallas kernels  39.8 us (96%)
  between operations  1.28 us (3%)
    pallas_call x1, Pallas kernels, body(): pl.pallas_call(kernel, out_shape=results, in_specs=[pl.BlockSpec(memory_s...  39.2 us

profile of v6, /device:TPU:8, one launch (start us, length us, event | category | flops | bytes accessed | tf_op | source)
XLA Modules:
  0.0 41.1 jit_solution(8888080209061873720)
XLA Ops:
  1.3 39.2 %shard_map.94 = (f32[2,4096]{1,0:T(2,128)S(1)}, f32[16,512]{1,0:T(8,128)S(1)}, f32[2,8]{1,0:T(2,128)S(1)}) custom-call(s32[1]{0:T(128)S(6)} %copy.10.length_ref, bf16[2,4096]{1,0:T(2,128)(2,1)} %bitcast.8, f32[128,1,512]{2,1,0:T(1,128)} %constant.4.clone.coarse_hbm, f32[32,512]{1,0:T(8,128)} %constant.5.clone.fine_hbm, bf16[1024,512]{1,0:T(8,128)(2,1)} %bitcast.7, ...), custom_call_target="tpu_custom_call" | custom-call | tf_op jit(solution)/shard_map/pallas_call | solution.py:442
  40.5 0.7 %shard_map.95 = (f32[2,4096]{1,0:T(2,128)}, f32[16,512]{1,0:T(8,128)}, f32[2,8]{1,0:T(2,128)}) custom-call(f32[2,4096]{1,0:T(2,128)S(1)} %get-tuple-element.9.refs_0_, f32[16,512]{1,0:T(8,128)S(1)} %get-tuple-element.10.refs_1_, f32[2,8]{1,0:T(2,128)S(1)} %get-tuple-element.11.refs_2_), custom_call_target="tpu_custom_call" | custom-call | tf_op jit(solution)/shard_map/pallas_call | solution.py:504
